TPU v7x, 32 devices: a whole 2x2x4 slice. The times are simulated.
32 devices in a mesh: shard: 4 (over y, x), ctx: 2 (over core), tp: 4 (over z).
Axes of the slice: x: 2, y: 2, z: 4, core: 2. Of those that a mesh axis runs over, the one named last changes fastest.
Arguments:
- latents: bfloat16 [4, 2048, 1024], P('shard', 'ctx'), may hold values from -6 to 6
- condition: bfloat16 [4, 1024], P('shard'), may hold values from -6 to 6
- modulation_weight: bfloat16 [1024, 6, 1024], P(('shard', 'ctx'), None, 'tp'), may hold values from -0.1875 to 0.1875
- modulation_bias: bfloat16 [6, 1024], P(None, 'tp'), may hold values from -3 to 3
- heads_weight: bfloat16 [1024, 3, 1024], P(('shard', 'ctx'), None, 'tp'), may hold values from -0.1875 to 0.1875
- heads_bias: bfloat16 [2, 1024], P(None, 'tp'), may hold values from -1.25 to 1.25
- merge_weight: bfloat16 [1024, 1024], P(('shard', 'ctx'), 'tp'), may hold values from -0.75 to 0.75
- merge_bias: bfloat16 [1024], replicated, may hold values from -3 to 3
- expand_weight: bfloat16 [1024, 4096], P(('shard', 'ctx'), 'tp'), may hold values from -0.1875 to 0.1875
- expand_bias: bfloat16 [4096], P('tp'), may hold values from -3 to 3
- reduce_weight: bfloat16 [1024, 4096], P(('shard', 'ctx'), 'tp'), may hold values from -0.09375 to 0.09375
- reduce_bias: bfloat16 [1024], replicated, may hold values from -3 to 3
- cotangent: bfloat16 [4, 2048, 1024], P('shard', 'ctx'), may hold values from -6 to 6
Outputs:
- output: bfloat16 [4, 2048, 1024], P('shard', 'ctx')
- latents_grad: float32 [4, 2048, 1024], P('shard', 'ctx')
- modulation_weight_grad: float32 [1024, 6, 1024], P(('shard', 'ctx'), None, 'tp')
- modulation_bias_grad: float32 [6, 1024], P(None, 'tp')
- heads_weight_grad: float32 [1024, 3, 1024], P(('shard', 'ctx'), None, 'tp')
- heads_bias_grad: float32 [2, 1024], P(None, 'tp')
- merge_weight_grad: float32 [1024, 1024], P(('shard', 'ctx'), 'tp')
- merge_bias_grad: float32 [1024], replicated
- expand_weight_grad: float32 [1024, 4096], P(('shard', 'ctx'), 'tp')
- expand_bias_grad: float32 [4096], P('tp')
- reduce_weight_grad: float32 [1024, 4096], P(('shard', 'ctx'), 'tp')
- reduce_bias_grad: float32 [1024], replicated
All inputs are finite; a program needn't handle non-finite values.
Results may differ from a plain program's by a relative error of at most 0.018.
The roundings to bfloat16 on the way count: a program that leaves them out, or rounds other values in their place, can miss the bound.
Values may be sent and summed in bfloat16 or wider, within the bound.
No kernel may reach another device: no remote copies, remote signals or barrier semaphores. Data moves between devices by JAX's collectives and lax.ppermute only.
A program may use at most 192 MiB of HBM per device.

v0:
```python
import jax
import jax.numpy as jnp
from jax import lax
from jax.sharding import PartitionSpec as P

HD = 64


def modulate(values, offset, scaling):
    centre = values - jnp.mean(values, axis=-1, keepdims=True)
    variance = jnp.mean(centre * centre, axis=-1, keepdims=True)
    normed = centre * lax.rsqrt(variance + 1e-06)
    return normed * (1.0 + scaling[:, None, :]) + offset[:, None, :]


def smooth_gate(values):
    return jax.nn.gelu(values, approximate=True)


def split_heads(queries, key_value):
    count = queries.shape[-1] // HD
    query_heads = queries.reshape(queries.shape[0], count, HD)
    key_heads = key_value[:, 0].reshape(key_value.shape[0], count, HD)
    value_heads = key_value[:, 1].reshape(key_value.shape[0], count, HD)
    scores = jnp.einsum(
        "qhd,khd->hqk", query_heads, key_heads, preferred_element_type=jnp.float32
    ) * HD ** (-0.5)
    return (query_heads, key_heads, value_heads, scores)


def attend(inputs):
    queries, key_value = inputs
    query_heads, key_heads, value_heads, scores = split_heads(queries, key_value)
    maximum_entry = jnp.max(scores, axis=-1, keepdims=True)
    exponent = jnp.exp(scores - maximum_entry)
    summed = jnp.sum(exponent, axis=-1, keepdims=True)
    attention = (exponent / summed).astype(jnp.bfloat16)
    blended_heads = jnp.einsum(
        "hqk,khd->qhd", attention, value_heads, preferred_element_type=jnp.float32
    )
    blended_heads = blended_heads.reshape(queries.shape[0], queries.shape[1]).astype(jnp.bfloat16)
    log_total = maximum_entry[..., 0] + jnp.log(summed[..., 0])
    return (blended_heads, log_total)


def attend_back(inputs):
    queries, key_value, mixture_grad, log_total = inputs
    query_heads, key_heads, value_heads, scores = split_heads(queries, key_value)
    grad_heads = mixture_grad.reshape(query_heads.shape)
    weights = jnp.exp(scores - log_total[..., None])
    attention = weights.astype(jnp.bfloat16)
    probs_grad = jnp.einsum(
        "qhd,khd->hqk", grad_heads, value_heads, preferred_element_type=jnp.float32
    )
    row_dot = jnp.sum(weights * probs_grad, axis=-1, keepdims=True)
    score_grad = (weights * (probs_grad - row_dot)).astype(jnp.bfloat16)
    query_grad = jnp.einsum(
        "hqk,khd->qhd", score_grad, key_heads, preferred_element_type=jnp.float32
    ) * HD ** (-0.5)
    key_grad = jnp.einsum(
        "hqk,qhd->khd", score_grad, query_heads, preferred_element_type=jnp.float32
    ) * HD ** (-0.5)
    value_grad = jnp.einsum(
        "hqk,qhd->khd", attention, grad_heads, preferred_element_type=jnp.float32
    )
    width = queries.shape[1]
    stacked = jnp.stack(
        [
            key_grad.reshape(key_value.shape[0], width),
            value_grad.reshape(key_value.shape[0], width),
        ],
        axis=1,
    )
    return (query_grad.reshape(queries.shape[0], width), stacked)


def body(
    latents,
    condition,
    modulation_weight,
    modulation_bias,
    heads_weight,
    heads_bias,
    merge_weight,
    merge_bias,
    expand_weight,
    expand_bias,
    reduce_weight,
    reduce_bias,
    cotangent,
):
    silu_condition = jax.nn.silu(condition.astype(jnp.float32)).astype(jnp.bfloat16)
    gathered = (
        lax.all_gather(modulation_weight, ("shard", "ctx"), axis=0, tiled=True),
        lax.all_gather(heads_weight, ("shard", "ctx"), axis=0, tiled=True),
        lax.all_gather(merge_weight, ("shard", "ctx"), axis=0, tiled=True),
        lax.all_gather(expand_weight, ("shard", "ctx"), axis=0, tiled=True),
        lax.all_gather(reduce_weight, ("shard", "ctx"), axis=0, tiled=True),
    )
    complete_modulation, heads_full, merge_complete, expand_full, reduce_full = gathered
    local_modulation = jnp.einsum(
        "ld,dkf->lkf", silu_condition, complete_modulation, preferred_element_type=jnp.float32
    )
    local_modulation = local_modulation + modulation_bias.astype(jnp.float32)
    modulation = lax.all_gather(local_modulation, "tp", axis=2, tiled=True)
    offset_one = modulation[:, 0]
    scaling_one = modulation[:, 1]
    gate_one = modulation[:, 2]
    offset_two = modulation[:, 3]
    scaling_two = modulation[:, 4]
    gate_two = modulation[:, 5]
    residual = latents.astype(jnp.float32)
    normed_one = modulate(residual, offset_one, scaling_one).astype(jnp.bfloat16)
    projected = jnp.einsum(
        "lsd,dkf->lskf", normed_one, heads_full, preferred_element_type=jnp.float32
    )
    bias_rows = heads_bias.astype(jnp.float32)
    bias_full = jnp.stack([bias_rows[0], jnp.zeros_like(bias_rows[0]), bias_rows[1]])
    projected = (projected + bias_full).astype(jnp.bfloat16)
    queries = projected[:, :, 0]
    key_value = lax.all_gather(projected[:, :, 1:], "ctx", axis=1, tiled=True)
    blended_heads, log_total = lax.map(attend, (queries, key_value))
    merged_output = jnp.einsum(
        "vzm,tm->vzt", blended_heads, merge_complete, preferred_element_type=jnp.float32
    )
    branch_one = lax.psum(merged_output.astype(jnp.bfloat16), "tp").astype(
        jnp.float32
    ) + merge_bias.astype(jnp.float32)
    middle = residual + gate_one[:, None, :] * branch_one
    normed_two = modulate(middle, offset_two, scaling_two).astype(jnp.bfloat16)
    hidden = jnp.einsum("lsd,dh->lsh", normed_two, expand_full, preferred_element_type=jnp.float32)
    hidden = hidden + expand_bias.astype(jnp.float32)
    activated = smooth_gate(hidden).astype(jnp.bfloat16)
    reduced = jnp.einsum("lsh,dh->lsd", activated, reduce_full, preferred_element_type=jnp.float32)
    branch_two = lax.psum(reduced.astype(jnp.bfloat16), "tp").astype(
        jnp.float32
    ) + reduce_bias.astype(jnp.float32)
    output = (middle + gate_two[:, None, :] * branch_two).astype(jnp.bfloat16)
    heads_back, merge_backward, expand_back, reduce_back = (
        lax.all_gather(heads_weight, ("shard", "ctx"), axis=0, tiled=True),
        lax.all_gather(merge_weight, ("shard", "ctx"), axis=0, tiled=True),
        lax.all_gather(expand_weight, ("shard", "ctx"), axis=0, tiled=True),
        lax.all_gather(reduce_weight, ("shard", "ctx"), axis=0, tiled=True),
    )
    upstream = cotangent.astype(jnp.float32)
    gate_two_grad = jnp.sum(upstream * branch_two, axis=1)
    branch_two_grad = (gate_two[:, None, :] * upstream).astype(jnp.bfloat16)
    reduce_bias_grad = jnp.sum(branch_two_grad.astype(jnp.float32), axis=(0, 1))
    reduce_weight_grad = jnp.einsum(
        "lsd,lsh->dh", branch_two_grad, activated, preferred_element_type=jnp.float32
    )
    activated_grad = jnp.einsum(
        "lsd,dh->lsh", branch_two_grad, reduce_back, preferred_element_type=jnp.float32
    )
    gate_pullback = jax.vjp(smooth_gate, hidden)[1]
    hidden_grad = gate_pullback(activated_grad)[0].astype(jnp.bfloat16)
    expand_bias_grad = jnp.sum(hidden_grad.astype(jnp.float32), axis=(0, 1))
    expand_weight_grad = jnp.einsum(
        "lsd,lsh->dh", normed_two, hidden_grad, preferred_element_type=jnp.float32
    )
    normed_two_part = jnp.einsum(
        "lsh,dh->lsd", hidden_grad, expand_back, preferred_element_type=jnp.float32
    )
    normed_two_grad = lax.psum(normed_two_part.astype(jnp.bfloat16), "tp").astype(jnp.float32)
    second_pullback = jax.vjp(modulate, middle, offset_two, scaling_two)[1]
    middle_part, offset_two_grad, scaling_two_grad = second_pullback(normed_two_grad)
    middle_grad = upstream + middle_part
    gate_one_grad = jnp.sum(middle_grad * branch_one, axis=1)
    first_branch_gradient = (gate_one[:, None, :] * middle_grad).astype(jnp.bfloat16)
    merge_bias_grad = jnp.sum(first_branch_gradient.astype(jnp.float32), axis=(0, 1))
    merge_weight_grad = jnp.einsum(
        "tab,tav->bv", first_branch_gradient, blended_heads, preferred_element_type=jnp.float32
    )
    mixture_grad = jnp.einsum(
        "yhq,qt->yht", first_branch_gradient, merge_backward, preferred_element_type=jnp.float32
    ).astype(jnp.bfloat16)
    query_grad, key_value_grad = lax.map(attend_back, (queries, key_value, mixture_grad, log_total))
    local_key_value = lax.psum_scatter(
        key_value_grad.astype(jnp.bfloat16), "ctx", scatter_dimension=1, tiled=True
    ).astype(jnp.float32)
    projected_grad = jnp.concatenate([query_grad[:, :, None], local_key_value], axis=2).astype(
        jnp.bfloat16
    )
    query_bias_grad = jnp.sum(projected_grad[:, :, 0].astype(jnp.float32), axis=(0, 1))
    value_bias_grad = jnp.sum(projected_grad[:, :, 2].astype(jnp.float32), axis=(0, 1))
    heads_bias_grad = jnp.stack([query_bias_grad, value_bias_grad])
    heads_weight_grad = jnp.einsum(
        "lsd,lskf->dkf", normed_one, projected_grad, preferred_element_type=jnp.float32
    )
    normed_one_part = jnp.einsum(
        "lskf,dkf->lsd", projected_grad, heads_back, preferred_element_type=jnp.float32
    )
    normed_one_grad = lax.psum(normed_one_part.astype(jnp.bfloat16), "tp").astype(jnp.float32)
    first_pullback = jax.vjp(modulate, residual, offset_one, scaling_one)[1]
    residual_part, offset_one_grad, scaling_one_grad = first_pullback(normed_one_grad)
    latents_grad = middle_grad + residual_part
    modulation_grad = jnp.stack(
        [
            offset_one_grad,
            scaling_one_grad,
            gate_one_grad,
            offset_two_grad,
            scaling_two_grad,
            gate_two_grad,
        ],
        axis=1,
    )
    feature_width = local_modulation.shape[2]
    local_grad = lax.dynamic_slice_in_dim(
        modulation_grad, lax.axis_index("tp") * feature_width, feature_width, 2
    )
    modulation_bias_grad = jnp.sum(local_grad, axis=0)
    condition_wide = silu_condition.astype(jnp.float32)
    modulation_weight_grad = jnp.einsum(
        "ld,lkf->dkf", condition_wide, local_grad, precision=lax.Precision.HIGHEST
    )
    weight_parts = (
        lax.psum_scatter(modulation_weight_grad, ("shard", "ctx"), scatter_dimension=0, tiled=True),
        lax.psum_scatter(heads_weight_grad, ("shard", "ctx"), scatter_dimension=0, tiled=True),
        lax.psum_scatter(merge_weight_grad, ("shard", "ctx"), scatter_dimension=0, tiled=True),
        lax.psum_scatter(expand_weight_grad, ("shard", "ctx"), scatter_dimension=0, tiled=True),
        lax.psum_scatter(reduce_weight_grad, ("shard", "ctx"), scatter_dimension=0, tiled=True),
    )
    modulation_rows_grad = weight_parts[0]
    heads_part, merge_part, expand_part, reduce_part = (
        weight_parts[1],
        weight_parts[2],
        weight_parts[3],
        weight_parts[4],
    )
    bias_parts = lax.psum(
        (
            modulation_bias_grad,
            heads_bias_grad,
            merge_bias_grad,
            expand_bias_grad,
            reduce_bias_grad,
        ),
        ("shard", "ctx"),
    )
    return (
        output,
        latents_grad,
        modulation_rows_grad,
        bias_parts[0],
        heads_part,
        bias_parts[1],
        merge_part,
        bias_parts[2],
        expand_part,
        bias_parts[3],
        reduce_part,
        bias_parts[4],
    )


def solution(mesh):
    return jax.shard_map(
        body,
        mesh=mesh,
        in_specs=(
            P("shard", "ctx", None),
            P("shard", None),
            P(("shard", "ctx"), None, "tp"),
            P(None, "tp"),
            P(("shard", "ctx"), None, "tp"),
            P(None, "tp"),
            P(("shard", "ctx"), "tp"),
            P(),
            P(("shard", "ctx"), "tp"),
            P("tp"),
            P(("shard", "ctx"), "tp"),
            P(),
            P("shard", "ctx", None),
        ),
        out_specs=(
            P("shard", "ctx", None),
            P("shard", "ctx", None),
            P(("shard", "ctx"), None, "tp"),
            P(None, "tp"),
            P(("shard", "ctx"), None, "tp"),
            P(None, "tp"),
            P(("shard", "ctx"), "tp"),
            P(),
            P(("shard", "ctx"), "tp"),
            P("tp"),
            P(("shard", "ctx"), "tp"),
            P(),
        ),
        check_vma=False,
    )
```

profile of v0, /device:TPU:0, one launch (start us, length us, event | category | flops | bytes accessed | tf_op | source)
XLA Modules:
  0.0 929.9 jit_solution(7180096306416691299)
XLA Ops:
  7.3 0.7 all-gather.7.cloned.1.call-update
  8.0 1.7 copy.25
  9.9 1.9 convert_reduce_fusion.2
  11.8 0.8 fusion.71
  12.7 0.7 fusion.23
  13.4 31.6 %all-gather.7.cloned.1.call-done = bf16[1024,6,256]{2,0,1:T(8,128)(2,1)} async-done(((bf16[128,6,256]{2,0,1:T(8,128)(2,1)}), bf16[1024,6,256]{2,0,1:T(8,128)(2,1)}) %all-gather.7.cloned.1.call-update) | async-done | bytes 3145744 | tf_op jit(solution)/shard_map/all_gather | solution.py:94
  45.0 2.4 fusion.56
  47.4 13.2 %all-gather = f32[6,1024]{1,0:T(8,128)S(1)} all-gather(f32[6,256]{1,0:T(8,128)S(1)} %bitcast_add_fusion), channel_id=2, replica_groups=mesh['shard'=4,'ctx'=2,'tp'=4] {'tp'}, dimensions={1}, use_global_device_ids=true | all-gather | bytes 30720 | tf_op jit(solution)/shard_map/all_gather | solution.py:105
  60.6 12.7 %all-gather.9.cloned.1.call-done = bf16[1024,3,256]{0,2,1:T(8,128)(2,1)} async-done(((bf16[128,3,256]{0,2,1:T(8,128)(2,1)}), bf16[1024,3,256]{0,2,1:T(8,128)(2,1)}) %all-gather.9.cloned.1.call-update) | async-done | bytes 1572880 | tf_op jit(solution)/shard_map/all_gather | solution.py:95
  73.4 3.4 fusion.49
  76.9 1.1 copy-done.16
  78.0 1.0 slice.65
  79.1 11.3 %all_gather.29 = bf16[1024,256]{1,0:T(8,128)(2,1)} all-gather(bf16[128,256]{1,0:T(8,128)(2,1)S(1)} %copy-done.22), channel_id=1, replica_groups=mesh['shard'=4,'ctx'=2,'tp'=4] {'shard','ctx'}, dimensions={0}, use_global_device_ids=true | all-gather | bytes 589824 | tf_op jit(solution)/shard_map/all_gather | solution.py:96
  90.4 1.1 slice.67
  91.5 2.9 fusion.69
  94.4 13.1 %multiply_reduce_fusion.1 = (f32[4,1024]{1,0:T(4,128)S(1)}, f32[4,1024,2048]{2,1,0:T(8,128)}) fusion(bf16[1024,4,64]{0,2,1:T(8,128)(2,1)S(1)} %bitcast.106, bf16[2048,4,64]{0,2,1:T(8,128)(2,1)S(1)} %bitcast.108), kind=kOutput, calls=%fused_computation.6 | convolution fusion | flops 1090514944 | bytes 35143680 | tf_op jit(solution)/shard_map/while/body/eval_jaxpr/qhd,khd->hqk/dot_general | solution.py:25
  107.5 14.1 %fusion = f32[4,1024]{1,0:T(4,128)S(1)} fusion(f32[4,1024,2048]{2,1,0:T(8,128)} %get-tuple-element.81, f32[4,1024]{1,0:T(4,128)S(1)} %get-tuple-element.80), kind=kLoop, calls=%fused_computation.5 | loop fusion | flops 25161728 | bytes 33587200 | tf_op jit(solution)/shard_map/while/body/eval_jaxpr/reduce_sum | solution.py:36
  121.6 15.0 %fusion.54 = bf16[4,64,1024]{2,1,0:T(8,128)(2,1)} fusion(bf16[2048,4,64]{0,2,1:T(8,128)(2,1)S(1)} %bitcast.110, f32[4,1024,2048]{2,1,0:T(8,128)} %get-tuple-element.81, f32[4,1024]{1,0:T(4,128)S(1)} %fusion, f32[4,1024]{1,0:T(4,128)S(1)} %get-tuple-element.80), kind=kOutput, calls=%fused_computation.89 | convolution fusion | flops 1107558400 | bytes 35160064 | tf_op jit(solution)/shard_map/while/body/eval_jaxpr/hqk,khd->qhd/dot_general | solution.py:38
  136.6 3.3 convert_bitcast_fusion.2
  141.4 85.3 %all-reduce.6.cloned.1.call-done = bf16[1,1024,1024]{2,1,0:T(8,128)(2,1)} async-done(((bf16[1,1024,1024]{2,1,0:T(8,128)(2,1)}), bf16[1,1024,1024]{2,1,0:T(8,128)(2,1)}) %all-reduce.6.cloned.1.call-update) | async-done | bytes 2097168 | tf_op jit(solution)/shard_map/psum | solution.py:126
  226.6 2.6 fusion.65
  229.3 1.2 multiply_reduce_fusion.3
  230.5 2.6 fusion.34
  233.1 22.3 %all-gather.13.cloned.1.call-done = bf16[1024,1024]{1,0:T(8,128)(2,1)} async-done(((bf16[128,1024]{1,0:T(8,128)(2,1)}), bf16[1024,1024]{1,0:T(8,128)(2,1)}) %all-gather.13.cloned.1.call-update) | async-done | bytes 2097168 | tf_op jit(solution)/shard_map/all_gather | solution.py:97
  255.4 6.6 fusion.72
  262.0 23.3 %all-gather.15.cloned.1.call-done = bf16[1024,1024]{1,0:T(8,128)(2,1)} async-done(((bf16[128,1024]{1,0:T(8,128)(2,1)}), bf16[1024,1024]{1,0:T(8,128)(2,1)}) %all-gather.15.cloned.1.call-update) | async-done | bytes 2097168 | tf_op jit(solution)/shard_map/all_gather | solution.py:98
  285.3 8.4 convert_reduce_fusion.4
  293.6 1.3 copy-done.36
  294.9 3.7 convert_bitcast_fusion
  298.9 86.4 %all-reduce.8.cloned.1.call-done = bf16[1,1024,1024]{2,1,0:T(8,128)(2,1)} async-done(((bf16[1,1024,1024]{2,1,0:T(8,128)(2,1)}), bf16[1,1024,1024]{2,1,0:T(8,128)(2,1)}) %all-reduce.8.cloned.1.call-update) | async-done | bytes 2097168 | tf_op jit(solution)/shard_map/psum | solution.py:164
  385.3 4.6 fusion.27
  390.0 2.5 fusion.68
  392.5 0.8 convert_reduce_fusion.5
  393.4 1.1 copy-done.4
  394.5 1.4 copy-done.8
  395.8 0.8 fusion.50
  396.6 14.7 %fusion.31 = bf16[4,64,2048]{2,1,0:T(8,128)(2,1)} fusion(bf16[1024,4,64]{0,2,1:T(8,128)(2,1)S(1)} %bitcast.114, f32[4,1024,2048]{2,1,0:T(8,128)} %get-tuple-element.81, f32[4,1024]{1,0:T(4,128)S(1)} %log_add_fusion), kind=kOutput, calls=%fused_computation.68 | convolution fusion | flops 1099431936 | bytes 35143680 | tf_op jit(solution)/shard_map/while/body/eval_jaxpr/hqk,qhd->khd/dot_general | solution.py:63
  411.3 22.3 %multiply_reduce_fusion = (f32[4,1024]{1,0:T(4,128)S(1)}, f32[4,1024,2048]{2,1,0:T(8,128)}) fusion(f32[4,1024,2048]{2,1,0:T(8,128)} %get-tuple-element.81, f32[4,1024]{1,0:T(4,128)S(1)} %log_add_fusion, bf16[1024,4,64]{0,2,1:T(8,128)(2,1)S(1)} %bitcast.115, bf16[2048,4,64]{0,2,1:T(8,128)(2,1)S(1)} %bitcast.111), kind=kOutput, calls=%fused_computation.1 | convolution fusion | flops 1107292160 | bytes 68714496 | tf_op jit(solution)/shard_map/while/body/eval_jaxpr/qhd,khd->hqk/dot_general | solution.py:52
  433.6 2.3 copy.27
  435.8 28.2 %multiply_convert_fusion = bf16[4,1024,2048]{2,1,0:T(8,128)(2,1)} fusion(f32[4,1024,2048]{2,1,0:T(8,128)} %get-tuple-element.83, f32[4,1024,2048]{2,1,0:T(8,128)} %get-tuple-element.81, f32[4,1024]{1,0:T(4,128)S(1)} %get-tuple-element.82, f32[4,1024]{1,0:T(4,128)S(1)} %log_add_fusion), kind=kLoop, calls=%fused_computation | loop fusion | flops 41943040 | bytes 83918848 | tf_op jit(solution)/shard_map/while/body/eval_jaxpr/convert_element_type | solution.py:56
  464.0 9.0 fusion.30
  473.0 1.3 copy.26
  474.3 3.0 pad_maximum_fusion
  477.4 7.1 convert_bitcast_fusion.1
  484.5 12.0 %convert_reduce_fusion.6 = (f32[4,64]{1,0:T(4,128)S(1)}, bf16[4,64,1024]{2,1,0:T(8,128)(2,1)}) fusion(bf16[2048,4,64]{0,2,1:T(8,128)(2,1)S(1)} %bitcast.109, bf16[4,1024,2048]{2,1,0:T(8,128)(2,1)} %multiply_convert_fusion), kind=kOutput, calls=%fused_computation.90 | convolution fusion | flops 1074790144 | bytes 18351104 | tf_op jit(solution)/shard_map/while/body/eval_jaxpr/hqk,khd->qhd/dot_general | solution.py:57
  496.5 1.2 copy.28
  497.8 4.9 fusion.46
  502.7 1.0 copy-done.14
  503.7 3.3 fusion.36
  507.3 7.0 fusion.73
  514.3 7.5 fusion.40
  521.9 0.6 copy-done.19
  522.5 5.0 fusion.55
  527.8 129.6 %all-reduce.10.cloned.1.call-done = (bf16[1,1024,1024]{2,1,0:T(8,128)(2,1)}, bf16[1,1024,1024]{2,1,0:T(8,128)(2,1)}) async-done(((bf16[1,1024,1024]{2,1,0:T(8,128)(2,1)}, bf16[1,1024,1024]{2,1,0:T(8,128)(2,1)}), (bf16[1,1024,1024]{2,1,0:T(8,128)(2,1)}, bf16[1,1024,1024]{2,1,0:T(8,128)(2,1)})) %all-reduce.10.cloned.1.call-update) | async-done | bytes 4194320 | tf_op jit(solution)/shard_map/psum | solution.py:135
  657.4 2.7 fusion.24
  660.1 2.6 fusion.28
  662.8 7.9 convert_reduce_fusion.3
  670.7 3.1 broadcast_multiply_fusion
  674.0 1.1 copy-done.17
  675.2 24.8 %all-reduce = (f32[6,256]{1,0:T(8,128)}, f32[2,256]{1,0:T(2,128)}, f32[1024]{0:T(1024)}, f32[1024]{0:T(1024)}, f32[1024]{0:T(1024)}) all-reduce(f32[6,256]{1,0:T(8,128)S(1)} %dynamic-slice_bitcast_fusion, f32[2,256]{1,0:T(2,128)S(1)} %pad_maximum_fusion.5, ...), channel_id=1, replica_groups=mesh['shard'=4,'ctx'=2,'tp'=4] {'shard','ctx'}, use_global_device_ids=true, to_apply=%region_23.24 | all-reduce | flops 5120 | bytes 40960 | tf_op jit(solution)/shard_map/psum | solution.py:231
  700.0 51.5 %reduce-scatter.15.cloned.1.call-done = f32[128,1024]{1,0:T(8,128)} async-done(((f32[1024,1024]{1,0:T(8,128)}), f32[128,1024]{1,0:T(8,128)}) %reduce-scatter.15.cloned.1.call-update) | async-done | bytes 524304 | tf_op jit(solution)/shard_map/reduce_scatter | solution.py:221
  751.5 55.5 %reduce-scatter.17.cloned.1.call-done = f32[128,1024]{1,0:T(8,128)} async-done(((f32[1024,1024]{1,0:T(8,128)}), f32[128,1024]{1,0:T(8,128)}) %reduce-scatter.17.cloned.1.call-update) | async-done | bytes 524304 | tf_op jit(solution)/shard_map/reduce_scatter | solution.py:222
  807.0 50.2 %reduce-scatter.11.cloned.1.call-done = f32[128,3,256]{2,0,1:T(8,128)} async-done(((f32[1024,3,256]{2,0,1:T(8,128)}), f32[128,3,256]{2,0,1:T(8,128)}) %reduce-scatter.11.cloned.1.call-update) | async-done | bytes 393232 | tf_op jit(solution)/shard_map/reduce_scatter | solution.py:219
  857.2 66.0 %reduce-scatter.9.cloned.1.call-done = f32[128,6,256]{2,0,1:T(8,128)} async-done(((f32[1024,6,256]{2,0,1:T(8,128)}), f32[128,6,256]{2,0,1:T(8,128)}) %reduce-scatter.9.cloned.1.call-update) | async-done | bytes 786448 | tf_op jit(solution)/shard_map/reduce_scatter | solution.py:218
  (120 shorter events, 3.2 us)
Async XLA Ops:
  7.2 5.5 copy-start
  7.2 37.8 %copy-start.27 = (bf16[1,1024]{1,0:T(2,128)(2,1)S(1)}, bf16[1,1024]{1,0:T(2,128)(2,1)}, u32[]{:S(2)}) copy-start(bf16[1,1024]{1,0:T(2,128)(2,1)} %param.14) | copy-start | bytes 6148
  7.2 40.2 %copy-start.31 = (bf16[6,256]{1,0:T(8,128)(2,1)S(1)}, bf16[6,256]{1,0:T(8,128)(2,1)}, u32[]{:S(2)}) copy-start(bf16[6,256]{1,0:T(8,128)(2,1)} %param.16) | copy-start | bytes 9220
  7.2 37.8 %all-gather.7.cloned.1.call-start = ((), (), s32[]{:S(2)}) async-start(), calls=%async_computation.6 | async-start | bytes 3538944 | tf_op jit(solution)/shard_map/all_gather | solution.py:94
  7.9 65.4 %all-gather.9.cloned.1.call-start = ((), (), s32[]{:S(2)}) async-start(), calls=%async_computation.7 | async-start | bytes 1769472 | tf_op jit(solution)/shard_map/all_gather | solution.py:95
  9.8 81.8 %all-gather.11.cloned.1.call-start = ((), (), s32[]{:S(2)}) async-start(), calls=%async_computation.8 | async-start | bytes 3145728 | tf_op jit(solution)/shard_map/all_gather | solution.py:121
  12.7 64.1 %copy-start.18 = (f32[1024]{0:T(1024)}, f32[1024]{0:T(1024)S(1)}, u32[]{:S(2)}) copy-start(f32[1024]{0:T(1024)S(1)} %broadcast_multiply_fusion.2) | copy-start | bytes 12292
  13.3 34.1 %copy-start.25 = (f32[1024]{0:T(1024)}, f32[1024]{0:T(1024)S(1)}, u32[]{:S(2)}) copy-start(f32[1024]{0:T(1024)S(1)} %fusion.23) | copy-start | bytes 12292
  13.4 63.4 %copy-start.23 = (f32[1024]{0:T(1024)}, f32[1024]{0:T(1024)S(1)}, u32[]{:S(2)}) copy-start(f32[1024]{0:T(1024)S(1)} %fusion.59) | copy-start | bytes 12292
  60.6 16.2 %copy-start.20 = (f32[1,1,1024]{2,1,0:T(1,128)}, f32[1,1,1024]{2,1,0:T(1,128)S(1)}, u32[]{:S(2)}) copy-start(f32[1,1,1024]{2,1,0:T(1,128)S(1)} %get-tuple-element.76) | copy-start | bytes 12292
  60.6 16.2 %copy-start.29 = (f32[1,1,1024]{2,1,0:T(1,128)}, f32[1,1,1024]{2,1,0:T(1,128)S(1)}, u32[]{:S(2)}) copy-start(f32[1,1,1024]{2,1,0:T(1,128)S(1)} %get-tuple-element.75) | copy-start | bytes 12292
  73.4 5.7 copy-start.22
  76.8 1.1 copy-start.16
  79.1 147.6 %all-reduce.6.cloned.1.call-start = ((), (), s32[]{:S(2)}) async-start(), calls=%async_computation.9 | async-start | bytes 4194304 | tf_op jit(solution)/shard_map/psum | solution.py:126
  91.5 16.0 %copy-start.6 = (bf16[1,1024,1,256]{1,3,2,0:T(8,128)(2,1)}, bf16[1,1024,1,256]{1,3,2,0:T(8,128)(2,1)S(1)}, u32[]{:S(2)}) copy-start(bf16[1,1024,1,256]{1,3,2,0:T(8,128)(2,1)S(1)} %slice.67) | copy-start | bytes 1572868
  94.4 13.1 %copy-start.9 = (bf16[2048,1,256]{0,2,1:T(8,128)(2,1)}, bf16[2048,1,256]{0,2,1:T(8,128)(2,1)S(1)}, u32[]{:S(2)}) copy-start(bf16[2048,1,256]{0,2,1:T(8,128)(2,1)S(1)} %get-tuple-element.70) | copy-start | bytes 3145732
  107.5 14.1 %copy-start.13 = (bf16[2048,1,256]{0,2,1:T(8,128)(2,1)S(1)}, bf16[2048,1,256]{0,2,1:T(8,128)(2,1)}, u32[]{:S(2)}) copy-start(bf16[2048,1,256]{0,2,1:T(8,128)(2,1)} %get-tuple-element.71) | copy-start | bytes 3145732
  136.6 4.7 copy-start.32
  136.6 4.7 copy-start.33
  139.9 115.5 %all-gather.13.cloned.1.call-start = ((), (), s32[]{:S(2)}) async-start(), calls=%async_computation.10 | async-start | bytes 2359296 | tf_op jit(solution)/shard_map/all_gather | solution.py:97
  140.5 144.7 %all-gather.15.cloned.1.call-start = ((), (), s32[]{:S(2)}) async-start(), calls=%async_computation.11 | async-start | bytes 2359296 | tf_op jit(solution)/shard_map/all_gather | solution.py:98
  141.1 244.2 %all-reduce.8.cloned.1.call-start = ((), (), s32[]{:S(2)}) async-start(), calls=%async_computation.12 | async-start | bytes 4194304 | tf_op jit(solution)/shard_map/psum | solution.py:164
  226.6 2.6 copy-start.1
  285.3 9.7 %copy-start.35 = (bf16[1024,1024]{1,0:T(8,128)(2,1)S(1)}, bf16[1024,1024]{1,0:T(8,128)(2,1)}, u32[]{:S(2)}) copy-start(bf16[1024,1024]{1,0:T(8,128)(2,1)} %all-gather.13.cloned.1.call-done) | copy-start | bytes 6291460
  293.6 1.3 copy-start.36
  298.6 199.2 %reduce-scatter.7.cloned.1.call-start = ((), (), s32[]{:S(2)}) async-start(), calls=%async_computation.13 | async-start | bytes 3145728 | tf_op jit(solution)/shard_map/reduce_scatter | solution.py:178
  385.3 4.6 copy-start.2
  385.3 4.6 copy-start.12
  390.0 2.6 copy-start.11
  392.5 2.0 copy-start.4
  392.5 3.3 copy-start.15
  394.5 1.4 copy-start.8
  477.4 7.2 copy-start.10
  477.4 180.0 %all-reduce.10.cloned.1.call-start = ((), (), s32[]{:S(2)}) async-start(), calls=%async_computation.19 | async-start | bytes 8388608 | tf_op jit(solution)/shard_map/psum | solution.py:135
  502.7 1.0 copy-start.14
  502.7 197.3 %reduce-scatter.13.cloned.1.call-start = ((), (), s32[]{:S(2)}) async-start(), calls=%async_computation.16 | async-start | bytes 1179648 | tf_op jit(solution)/shard_map/reduce_scatter | solution.py:220
  507.1 244.4 %reduce-scatter.15.cloned.1.call-start = ((), (), s32[]{:S(2)}) async-start(), calls=%async_computation.17 | async-start | bytes 4718592 | tf_op jit(solution)/shard_map/reduce_scatter | solution.py:221
  514.3 292.7 %reduce-scatter.17.cloned.1.call-start = ((), (), s32[]{:S(2)}) async-start(), calls=%async_computation.18 | async-start | bytes 4718592 | tf_op jit(solution)/shard_map/reduce_scatter | solution.py:222
  521.8 0.7 copy-start.19
  521.8 0.7 copy-start.21
  521.8 0.7 copy-start.24
  521.8 0.7 copy-start.30
  521.9 5.8 copy-start.28
  521.9 5.9 copy-start.34
  521.9 335.3 %reduce-scatter.11.cloned.1.call-start = ((), (), s32[]{:S(2)}) async-start(), calls=%async_computation.15 | async-start | bytes 3538944 | tf_op jit(solution)/shard_map/reduce_scatter | solution.py:219
  527.6 132.5 %copy-start.26 = (f32[1024]{0:T(1024)S(1)}, f32[1024]{0:T(1024)}, u32[]{:S(2)}) copy-start(f32[1024]{0:T(1024)} %copy-done.25) | copy-start | bytes 12292
  527.6 395.6 %reduce-scatter.9.cloned.1.call-start = ((), (), s32[]{:S(2)}) async-start(), calls=%async_computation.14 | async-start | bytes 7077888 | tf_op jit(solution)/shard_map/reduce_scatter | solution.py:218
  657.4 2.8 copy-start.7
  657.4 5.4 copy-start.3
  657.4 5.4 copy-start.5
  673.9 1.2 copy-start.17
Sparse Core Ops, SparseCore 0:
  9.9 35.0 all-gather.6
  47.4 25.8 all-gather.8
  79.2 10.5 all-gather.10
  140.1 86.5 all-reduce.5
  228.5 26.8 all-gather.12
  257.3 27.8 all-gather.14
  298.8 86.5 all-reduce.7
  477.5 8.5 reduce-scatter.6
  502.8 154.5 all-reduce.9
  661.0 35.2 reduce-scatter.12
  700.2 51.2 reduce-scatter.14
  755.6 51.2 reduce-scatter.16
  810.9 46.2 reduce-scatter.10
  861.4 61.7 reduce-scatter.8
where the time goes:
time: 934 us; the launch traced here: 930 us
  waiting for transfers between devices  616 us (66%)
  matrix products  149 us (16%)
  other arithmetic  79 us (8%)
  blocking collectives  49.2 us (5%)
  local copies, waits for them, and re-layouts  20.2 us (2%)
  between operations  14.6 us (2%)
    psum x1, waiting for transfers between devices, body(): lax.psum(reduced.astype(jnp.bfloat16), 'tp').astype(jnp.float32)  130 us
    psum x1, waiting for transfers between devices, body(): lax.psum(normed_two_part.astype(jnp.bfloat16), 'tp').astype(jnp.float32)  86.4 us
    psum x1, waiting for transfers between devices, body(): lax.psum(merged_output.astype(jnp.bfloat16), 'tp').astype(jnp.float32)  85.3 us
    reduce_scatter x1, waiting for transfers between devices, body(): lax.psum_scatter(modulation_weight_grad, ('shard', 'ctx'), scatter_dimens...  66 us
    reduce_scatter x1, waiting for transfers between devices, body(): lax.psum_scatter(reduce_weight_grad, ('shard', 'ctx'), scatter_dimension=...  55.5 us
    reduce_scatter x1, waiting for transfers between devices, body(): lax.psum_scatter(expand_weight_grad, ('shard', 'ctx'), scatter_dimension=...  51.5 us
    reduce_scatter x1, waiting for transfers between devices, body(): lax.psum_scatter(heads_weight_grad, ('shard', 'ctx'), scatter_dimension=0...  50.2 us
    all_gather x1, waiting for transfers between devices, body(): lax.all_gather(modulation_weight, ('shard', 'ctx'), axis=0, tiled=True)  31.6 us
  transfers between devices with their start and end apart: 14, of which 11 were waited for; matrix products, arithmetic and copies ran while one was open for 9% of the time, Pallas kernels for 0%

commit v1 on v0

--- a/solution.py
+++ b/solution.py
@@ -2,8 +2,13 @@
 import jax.numpy as jnp
 from jax import lax
 from jax.sharding import PartitionSpec as P
+from jax.lax import all_gather
 
 HD = 64
+
+
+def stages_all_meet(panel):
+    return all_gather(panel, axis_name="tp").sum(axis=0)
 
 
 def modulate(values, offset, scaling):
@@ -132,7 +137,7 @@
     hidden = hidden + expand_bias.astype(jnp.float32)
     activated = smooth_gate(hidden).astype(jnp.bfloat16)
     reduced = jnp.einsum("lsh,dh->lsd", activated, reduce_full, preferred_element_type=jnp.float32)
-    branch_two = lax.psum(reduced.astype(jnp.bfloat16), "tp").astype(
+    branch_two = stages_all_meet(reduced.astype(jnp.bfloat16)).astype(
         jnp.float32
     ) + reduce_bias.astype(jnp.float32)
     output = (middle + gate_two[:, None, :] * branch_two).astype(jnp.bfloat16)

time: 934 us -> 1010 us (1.081)
  waiting for transfers between devices: 616 us -> 684 us
  other arithmetic: 79 us -> 91.1 us
    all_gather x0 -> x1, waiting for transfers between devices: none -> 142 us  [stages_all_meet(): return all_gather(panel, axis_name='tp').sum(axis=0)]
    psum x1, waiting for transfers between devices: 130 us -> 60.7 us  [body(): lax.psum(normed_one_part.astype(jnp.bfloat16), 'tp').astype(jnp.float32)]
    reduce_scatter x1, waiting for transfers between devices: 0.01 us -> 39.8 us  [body(): lax.psum_scatter(merge_weight_grad, ('shard', 'ctx'), scatter_dimension=0...]
    reduce_scatter x1, waiting for transfers between devices: 51.5 us -> 13.7 us  [body(): lax.psum_scatter(expand_weight_grad, ('shard', 'ctx'), scatter_dimension=...]
  transfers between devices with their start and end apart: 14 -> 15, of which waited for: 11 -> 13; matrix products, arithmetic and copies ran while one was open for 9% -> 9% of each run, Pallas kernels for 0% -> 0%
where the time goes in v1:
time: 1010 us
  waiting for transfers between devices  684 us (68%)
  matrix products  150 us (15%)
  other arithmetic  91.1 us (9%)
  blocking collectives  49.4 us (5%)
  local copies, waits for them, and re-layouts  19.1 us (2%)
  between operations  14.6 us (1%)
    all_gather x1, waiting for transfers between devices, stages_all_meet(): return all_gather(panel, axis_name='tp').sum(axis=0)  142 us
    psum x1, waiting for transfers between devices, body(): lax.psum(merged_output.astype(jnp.bfloat16), 'tp').astype(jnp.float32)  85.3 us
    psum x1, waiting for transfers between devices, body(): lax.psum(normed_two_part.astype(jnp.bfloat16), 'tp').astype(jnp.float32)  79.3 us
    reduce_scatter x1, waiting for transfers between devices, body(): lax.psum_scatter(modulation_weight_grad, ('shard', 'ctx'), scatter_dimens...  65.9 us
    psum x1, waiting for transfers between devices, body(): lax.psum(normed_one_part.astype(jnp.bfloat16), 'tp').astype(jnp.float32)  60.7 us
    reduce_scatter x1, waiting for transfers between devices, body(): lax.psum_scatter(reduce_weight_grad, ('shard', 'ctx'), scatter_dimension=...  55.5 us
    reduce_scatter x1, waiting for transfers between devices, body(): lax.psum_scatter(heads_weight_grad, ('shard', 'ctx'), scatter_dimension=0...  50 us
    reduce_scatter x1, waiting for transfers between devices, body(): lax.psum_scatter(merge_weight_grad, ('shard', 'ctx'), scatter_dimension=0...  39.8 us
  transfers between devices with their start and end apart: 15, of which 13 were waited for; matrix products, arithmetic and copies ran while one was open for 9% of the time, Pallas kernels for 0%

profile of v1, /device:TPU:0, one launch (start us, length us, event | category | flops | bytes accessed | tf_op | source)
XLA Modules:
  0.0 1008.7 jit_solution(7253822820920419945)
XLA Ops:
  8.0 1.7 copy.25
  9.9 1.9 convert_reduce_fusion.2
  11.8 0.8 fusion.74
  12.7 0.7 fusion.23
  14.0 31.0 %all-gather.9.cloned.1.call-done = bf16[1024,6,256]{2,0,1:T(8,128)(2,1)} async-done(((bf16[128,6,256]{2,0,1:T(8,128)(2,1)}), bf16[1024,6,256]{2,0,1:T(8,128)(2,1)}) %all-gather.9.cloned.1.call-update) | async-done | bytes 3145744 | tf_op jit(solution)/shard_map/all_gather | solution.py:99
  45.0 2.4 fusion.59
  47.4 13.1 %all-gather = f32[6,1024]{1,0:T(8,128)S(1)} all-gather(f32[6,256]{1,0:T(8,128)S(1)} %bitcast_add_fusion), channel_id=2, replica_groups=mesh['shard'=4,'ctx'=2,'tp'=4] {'tp'}, dimensions={1}, use_global_device_ids=true | all-gather | bytes 30720 | tf_op jit(solution)/shard_map/all_gather | solution.py:110
  60.6 12.8 %all-gather.11.cloned.1.call-done = bf16[1024,3,256]{0,2,1:T(8,128)(2,1)} async-done(((bf16[128,3,256]{0,2,1:T(8,128)(2,1)}), bf16[1024,3,256]{0,2,1:T(8,128)(2,1)}) %all-gather.11.cloned.1.call-update) | async-done | bytes 1572880 | tf_op jit(solution)/shard_map/all_gather | solution.py:100
  73.4 3.4 fusion.52
  76.9 1.1 copy-done.12
  78.0 1.0 slice.65
  79.1 11.3 %all_gather.35 = bf16[1024,256]{1,0:T(8,128)(2,1)} all-gather(bf16[128,256]{1,0:T(8,128)(2,1)S(1)} %copy-done.16), channel_id=1, replica_groups=mesh['shard'=4,'ctx'=2,'tp'=4] {'shard','ctx'}, dimensions={0}, use_global_device_ids=true | all-gather | bytes 589824 | tf_op jit(solution)/shard_map/all_gather | solution.py:101
  90.4 1.1 slice.67
  91.5 2.9 fusion.72
  94.4 13.1 %multiply_reduce_fusion.1 = (f32[4,1024]{1,0:T(4,128)S(1)}, f32[4,1024,2048]{2,1,0:T(8,128)}) fusion(bf16[1024,4,64]{0,2,1:T(8,128)(2,1)S(1)} %bitcast.109, bf16[2048,4,64]{0,2,1:T(8,128)(2,1)S(1)} %bitcast.111), kind=kOutput, calls=%fused_computation.6 | convolution fusion | flops 1090514944 | bytes 35143680 | tf_op jit(solution)/shard_map/while/body/eval_jaxpr/qhd,khd->hqk/dot_general | solution.py:30
  107.5 14.1 %fusion = f32[4,1024]{1,0:T(4,128)S(1)} fusion(f32[4,1024,2048]{2,1,0:T(8,128)} %get-tuple-element.80, f32[4,1024]{1,0:T(4,128)S(1)} %get-tuple-element.79), kind=kLoop, calls=%fused_computation.5 | loop fusion | flops 25161728 | bytes 33587200 | tf_op jit(solution)/shard_map/while/body/eval_jaxpr/reduce_sum | solution.py:41
  121.6 15.0 %fusion.57 = bf16[4,64,1024]{2,1,0:T(8,128)(2,1)} fusion(bf16[2048,4,64]{0,2,1:T(8,128)(2,1)S(1)} %bitcast.114, f32[4,1024,2048]{2,1,0:T(8,128)} %get-tuple-element.80, f32[4,1024]{1,0:T(4,128)S(1)} %fusion, f32[4,1024]{1,0:T(4,128)S(1)} %get-tuple-element.79), kind=kOutput, calls=%fused_computation.91 | convolution fusion | flops 1107558400 | bytes 35160064 | tf_op jit(solution)/shard_map/while/body/eval_jaxpr/hqk,khd->qhd/dot_general | solution.py:43
  136.5 3.3 convert_bitcast_fusion.1
  141.3 85.3 %all-reduce.5.cloned.1.call-done = bf16[1,1024,1024]{2,1,0:T(8,128)(2,1)} async-done(((bf16[1,1024,1024]{2,1,0:T(8,128)(2,1)}), bf16[1,1024,1024]{2,1,0:T(8,128)(2,1)}) %all-reduce.5.cloned.1.call-update) | async-done | bytes 2097168 | tf_op jit(solution)/shard_map/psum | solution.py:131
  226.6 2.6 fusion.68
  229.2 1.2 multiply_reduce_fusion.3
  230.4 2.7 fusion.37
  233.1 22.2 %all-gather.15.cloned.1.call-done = bf16[1024,1024]{1,0:T(8,128)(2,1)} async-done(((bf16[128,1024]{1,0:T(8,128)(2,1)}), bf16[1024,1024]{1,0:T(8,128)(2,1)}) %all-gather.15.cloned.1.call-update) | async-done | bytes 2097168 | tf_op jit(solution)/shard_map/all_gather | solution.py:102
  255.4 6.6 fusion.75
  261.9 23.3 %all-gather.17.cloned.1.call-done = bf16[1024,1024]{1,0:T(8,128)(2,1)} async-done(((bf16[128,1024]{1,0:T(8,128)(2,1)}), bf16[1024,1024]{1,0:T(8,128)(2,1)}) %all-gather.17.cloned.1.call-update) | async-done | bytes 2097168 | tf_op jit(solution)/shard_map/all_gather | solution.py:103
  285.2 8.4 convert_reduce_fusion.4
  293.6 1.3 copy-done.32
  294.9 3.7 convert_bitcast_fusion
  298.9 7.0 convolution_convert_fusion
  305.9 79.3 %all-reduce.7.cloned.1.call-done = bf16[1,1024,1024]{2,1,0:T(8,128)(2,1)} async-done(((bf16[1,1024,1024]{2,1,0:T(8,128)(2,1)}), bf16[1,1024,1024]{2,1,0:T(8,128)(2,1)}) %all-reduce.7.cloned.1.call-update) | async-done | bytes 2097168 | tf_op jit(solution)/shard_map/psum | solution.py:169
  385.3 4.2 fusion.27
  389.5 3.8 fusion.71
  393.3 142.1 %all-gather.19.cloned.1.call-done = bf16[4096,1024]{1,0:T(8,128)(2,1)} async-done(((bf16[1024,1024]{1,0:T(8,128)(2,1)}), bf16[4096,1024]{1,0:T(8,128)(2,1)}) %all-gather.19.cloned.1.call-update) | async-done | bytes 8388624 | tf_op jit(solution)/shard_map/all_gather | solution.py:11
  535.4 7.4 reduce.22
  542.9 6.9 convert_reduce_fusion.3
  549.8 1.4 copy-done.5
  551.1 0.8 fusion.53
  551.9 14.7 %fusion.34 = bf16[4,64,2048]{2,1,0:T(8,128)(2,1)} fusion(bf16[1024,4,64]{0,2,1:T(8,128)(2,1)S(1)} %bitcast.118, f32[4,1024,2048]{2,1,0:T(8,128)} %get-tuple-element.80, f32[4,1024]{1,0:T(4,128)S(1)} %log_add_fusion), kind=kOutput, calls=%fused_computation.70 | convolution fusion | flops 1099431936 | bytes 35143680 | tf_op jit(solution)/shard_map/while/body/eval_jaxpr/hqk,qhd->khd/dot_general | solution.py:68
  566.6 22.8 %multiply_reduce_fusion = (f32[4,1024]{1,0:T(4,128)S(1)}, f32[4,1024,2048]{2,1,0:T(8,128)}) fusion(f32[4,1024,2048]{2,1,0:T(8,128)} %get-tuple-element.80, f32[4,1024]{1,0:T(4,128)S(1)} %log_add_fusion, bf16[1024,4,64]{0,2,1:T(8,128)(2,1)S(1)} %bitcast.119, bf16[2048,4,64]{0,2,1:T(8,128)(2,1)S(1)} %bitcast.115), kind=kOutput, calls=%fused_computation.1 | convolution fusion | flops 1107292160 | bytes 68714496 | tf_op jit(solution)/shard_map/while/body/eval_jaxpr/qhd,khd->hqk/dot_general | solution.py:57
  589.3 2.3 copy.27
  591.6 27.8 %multiply_convert_fusion = bf16[4,1024,2048]{2,1,0:T(8,128)(2,1)} fusion(f32[4,1024,2048]{2,1,0:T(8,128)} %get-tuple-element.82, f32[4,1024,2048]{2,1,0:T(8,128)} %get-tuple-element.80, f32[4,1024]{1,0:T(4,128)S(1)} %get-tuple-element.81, f32[4,1024]{1,0:T(4,128)S(1)} %log_add_fusion), kind=kLoop, calls=%fused_computation | loop fusion | flops 41943040 | bytes 83918848 | tf_op jit(solution)/shard_map/while/body/eval_jaxpr/convert_element_type | solution.py:61
  619.4 9.0 fusion.33
  628.4 1.3 copy.26
  629.7 3.2 pad_maximum_fusion
  633.0 12.5 %convert_reduce_fusion.6 = (f32[4,64]{1,0:T(4,128)S(1)}, bf16[4,64,1024]{2,1,0:T(8,128)(2,1)}) fusion(bf16[2048,4,64]{0,2,1:T(8,128)(2,1)S(1)} %bitcast.112, bf16[4,1024,2048]{2,1,0:T(8,128)(2,1)} %multiply_convert_fusion), kind=kOutput, calls=%fused_computation.92 | convolution fusion | flops 1074790144 | bytes 18351104 | tf_op jit(solution)/shard_map/while/body/eval_jaxpr/hqk,khd->qhd/dot_general | solution.py:62
  645.4 1.2 copy.28
  646.7 4.9 fusion.49
  651.8 6.6 fusion.76
  658.6 7.5 fusion.43
  666.1 0.9 copy-done.10
  667.0 3.4 fusion.39
  670.5 5.0 fusion.58
  675.7 60.7 %all-reduce.9.cloned.1.call-done = bf16[1,1024,1024]{2,1,0:T(8,128)(2,1)} async-done(((bf16[1,1024,1024]{2,1,0:T(8,128)(2,1)}), bf16[1,1024,1024]{2,1,0:T(8,128)(2,1)}) %all-reduce.9.cloned.1.call-update) | async-done | bytes 2097168 | tf_op jit(solution)/shard_map/psum | solution.py:198
  736.4 2.7 fusion.24
  739.2 2.6 fusion.28
  741.8 3.1 broadcast_multiply_fusion
  745.1 1.1 copy-done.13
  746.4 25.0 %all-reduce = (f32[6,256]{1,0:T(8,128)}, f32[2,256]{1,0:T(2,128)}, f32[1024]{0:T(1024)}, f32[1024]{0:T(1024)}, f32[1024]{0:T(1024)}) all-reduce(f32[6,256]{1,0:T(8,128)S(1)} %dynamic-slice_bitcast_fusion, f32[2,256]{1,0:T(2,128)S(1)} %pad_maximum_fusion.5, ...), channel_id=1, replica_groups=mesh['shard'=4,'ctx'=2,'tp'=4] {'shard','ctx'}, use_global_device_ids=true, to_apply=%region_23.24 | all-reduce | flops 5120 | bytes 40960 | tf_op jit(solution)/shard_map/psum | solution.py:236
  771.3 5.8 add_add_fusion.2
  777.1 13.7 %reduce-scatter.15.cloned.1.call-done = f32[128,1024]{1,0:T(8,128)} async-done(((f32[1024,1024]{1,0:T(8,128)}), f32[128,1024]{1,0:T(8,128)}) %reduce-scatter.15.cloned.1.call-update) | async-done | bytes 524304 | tf_op jit(solution)/shard_map/reduce_scatter | solution.py:226
  790.8 55.5 %reduce-scatter.17.cloned.1.call-done = f32[128,1024]{1,0:T(8,128)} async-done(((f32[1024,1024]{1,0:T(8,128)}), f32[128,1024]{1,0:T(8,128)}) %reduce-scatter.17.cloned.1.call-update) | async-done | bytes 524304 | tf_op jit(solution)/shard_map/reduce_scatter | solution.py:227
  846.3 39.8 %reduce-scatter.13.cloned.1.call-done = f32[128,256]{1,0:T(8,128)} async-done(((f32[1024,256]{1,0:T(8,128)}), f32[128,256]{1,0:T(8,128)}) %reduce-scatter.13.cloned.1.call-update) | async-done | bytes 131088 | tf_op jit(solution)/shard_map/reduce_scatter | solution.py:225
  886.0 50.0 %reduce-scatter.11.cloned.1.call-done = f32[128,3,256]{2,0,1:T(8,128)} async-done(((f32[1024,3,256]{2,0,1:T(8,128)}), f32[128,3,256]{2,0,1:T(8,128)}) %reduce-scatter.11.cloned.1.call-update) | async-done | bytes 393232 | tf_op jit(solution)/shard_map/reduce_scatter | solution.py:224
  936.1 65.9 %reduce-scatter.9.cloned.1.call-done = f32[128,6,256]{2,0,1:T(8,128)} async-done(((f32[1024,6,256]{2,0,1:T(8,128)}), f32[128,6,256]{2,0,1:T(8,128)}) %reduce-scatter.9.cloned.1.call-update) | async-done | bytes 786448 | tf_op jit(solution)/shard_map/reduce_scatter | solution.py:223
  (116 shorter events, 4.5 us)
Async XLA Ops:
  7.2 5.5 copy-start
  7.2 37.8 %copy-start.23 = (bf16[1,1024]{1,0:T(2,128)(2,1)S(1)}, bf16[1,1024]{1,0:T(2,128)(2,1)}, u32[]{:S(2)}) copy-start(bf16[1,1024]{1,0:T(2,128)(2,1)} %param.14) | copy-start | bytes 6148
  7.2 40.2 %copy-start.27 = (bf16[6,256]{1,0:T(8,128)(2,1)S(1)}, bf16[6,256]{1,0:T(8,128)(2,1)}, u32[]{:S(2)}) copy-start(bf16[6,256]{1,0:T(8,128)(2,1)} %param.16) | copy-start | bytes 9220
  7.2 37.8 %all-gather.9.cloned.1.call-start = ((), (), s32[]{:S(2)}) async-start(), calls=%async_computation.6 | async-start | bytes 3538944 | tf_op jit(solution)/shard_map/all_gather | solution.py:99
  7.9 65.4 %all-gather.11.cloned.1.call-start = ((), (), s32[]{:S(2)}) async-start(), calls=%async_computation.7 | async-start | bytes 1769472 | tf_op jit(solution)/shard_map/all_gather | solution.py:100
  9.8 81.7 %all-gather.13.cloned.1.call-start = ((), (), s32[]{:S(2)}) async-start(), calls=%async_computation.8 | async-start | bytes 3145728 | tf_op jit(solution)/shard_map/all_gather | solution.py:126
  12.7 64.1 %copy-start.14 = (f32[1024]{0:T(1024)}, f32[1024]{0:T(1024)S(1)}, u32[]{:S(2)}) copy-start(f32[1024]{0:T(1024)S(1)} %broadcast_multiply_fusion.2) | copy-start | bytes 12292
  13.3 0.6 copy-start.19
  14.0 62.9 %copy-start.21 = (f32[1024]{0:T(1024)}, f32[1024]{0:T(1024)S(1)}, u32[]{:S(2)}) copy-start(f32[1024]{0:T(1024)S(1)} %fusion.62) | copy-start | bytes 12292
  60.6 16.2 %copy-start.17 = (f32[1,1,1024]{2,1,0:T(1,128)}, f32[1,1,1024]{2,1,0:T(1,128)S(1)}, u32[]{:S(2)}) copy-start(f32[1,1,1024]{2,1,0:T(1,128)S(1)} %get-tuple-element.75) | copy-start | bytes 12292
  60.6 16.2 %copy-start.25 = (f32[1,1,1024]{2,1,0:T(1,128)}, f32[1,1,1024]{2,1,0:T(1,128)S(1)}, u32[]{:S(2)}) copy-start(f32[1,1,1024]{2,1,0:T(1,128)S(1)} %get-tuple-element.74) | copy-start | bytes 12292
  73.4 5.7 copy-start.16
  76.8 1.1 copy-start.12
  79.1 147.5 %all-reduce.5.cloned.1.call-start = ((), (), s32[]{:S(2)}) async-start(), calls=%async_computation.9 | async-start | bytes 4194304 | tf_op jit(solution)/shard_map/psum | solution.py:131
  91.4 16.0 %copy-start.3 = (bf16[1,1024,1,256]{1,3,2,0:T(8,128)(2,1)}, bf16[1,1024,1,256]{1,3,2,0:T(8,128)(2,1)S(1)}, u32[]{:S(2)}) copy-start(bf16[1,1024,1,256]{1,3,2,0:T(8,128)(2,1)S(1)} %slice.67) | copy-start | bytes 1572868
  94.4 13.1 %copy-start.6 = (bf16[2048,1,256]{0,2,1:T(8,128)(2,1)}, bf16[2048,1,256]{0,2,1:T(8,128)(2,1)S(1)}, u32[]{:S(2)}) copy-start(bf16[2048,1,256]{0,2,1:T(8,128)(2,1)S(1)} %get-tuple-element.69) | copy-start | bytes 3145732
  107.5 14.1 %copy-start.9 = (bf16[2048,1,256]{0,2,1:T(8,128)(2,1)S(1)}, bf16[2048,1,256]{0,2,1:T(8,128)(2,1)}, u32[]{:S(2)}) copy-start(bf16[2048,1,256]{0,2,1:T(8,128)(2,1)} %get-tuple-element.70) | copy-start | bytes 3145732
  136.5 4.7 copy-start.28
  136.5 4.7 copy-start.29
  139.9 115.5 %all-gather.15.cloned.1.call-start = ((), (), s32[]{:S(2)}) async-start(), calls=%async_computation.10 | async-start | bytes 2359296 | tf_op jit(solution)/shard_map/all_gather | solution.py:102
  140.5 144.7 %all-gather.17.cloned.1.call-start = ((), (), s32[]{:S(2)}) async-start(), calls=%async_computation.11 | async-start | bytes 2359296 | tf_op jit(solution)/shard_map/all_gather | solution.py:103
  141.0 244.2 %all-reduce.7.cloned.1.call-start = ((), (), s32[]{:S(2)}) async-start(), calls=%async_computation.12 | async-start | bytes 4194304 | tf_op jit(solution)/shard_map/psum | solution.py:169
  226.6 2.6 copy-start.1
  285.2 9.7 copy-start.31
  293.6 1.3 copy-start.32
  298.6 7.3 copy-start.30
  298.6 236.9 %all-gather.19.cloned.1.call-start = ((), (), s32[]{:S(2)}) async-start(), calls=%async_computation.20 | async-start | bytes 10485760 | tf_op jit(solution)/shard_map/all_gather | solution.py:11
  305.8 340.9 %reduce-scatter.7.cloned.1.call-start = ((), (), s32[]{:S(2)}) async-start(), calls=%async_computation.13 | async-start | bytes 3145728 | tf_op jit(solution)/shard_map/reduce_scatter | solution.py:183
  385.3 4.3 copy-start.2
  385.3 4.3 copy-start.8
  542.9 8.2 copy-start.11
  549.8 1.4 copy-start.5
  629.7 3.3 copy-start.7
  632.9 103.5 %all-reduce.9.cloned.1.call-start = ((), (), s32[]{:S(2)}) async-start(), calls=%async_computation.14 | async-start | bytes 4194304 | tf_op jit(solution)/shard_map/psum | solution.py:198
  651.6 139.1 %reduce-scatter.15.cloned.1.call-start = ((), (), s32[]{:S(2)}) async-start(), calls=%async_computation.18 | async-start | bytes 4718592 | tf_op jit(solution)/shard_map/reduce_scatter | solution.py:226
  658.5 187.8 %reduce-scatter.17.cloned.1.call-start = ((), (), s32[]{:S(2)}) async-start(), calls=%async_computation.19 | async-start | bytes 4718592 | tf_op jit(solution)/shard_map/reduce_scatter | solution.py:227
  666.0 1.0 copy-start.10
  666.0 4.5 copy-start.15
  666.0 4.5 copy-start.18
  666.1 4.5 copy-start.22
  666.1 4.5 copy-start.26
  666.1 220.0 %reduce-scatter.13.cloned.1.call-start = ((), (), s32[]{:S(2)}) async-start(), calls=%async_computation.17 | async-start | bytes 1179648 | tf_op jit(solution)/shard_map/reduce_scatter | solution.py:225
  670.4 5.2 copy-start.24
  670.4 265.6 %reduce-scatter.11.cloned.1.call-start = ((), (), s32[]{:S(2)}) async-start(), calls=%async_computation.16 | async-start | bytes 3538944 | tf_op jit(solution)/shard_map/reduce_scatter | solution.py:224
  675.6 63.6 %copy-start.20 = (f32[1024]{0:T(1024)S(1)}, f32[1024]{0:T(1024)}, u32[]{:S(2)}) copy-start(f32[1024]{0:T(1024)} %copy-done.19) | copy-start | bytes 12292
  675.6 326.4 %reduce-scatter.9.cloned.1.call-start = ((), (), s32[]{:S(2)}) async-start(), calls=%async_computation.15 | async-start | bytes 7077888 | tf_op jit(solution)/shard_map/reduce_scatter | solution.py:223
  736.4 2.7 copy-start.4
  745.0 1.2 copy-start.13
Sparse Core Ops, SparseCore 0:
  9.9 35.0 all-gather.8
  47.4 25.8 all-gather.10
  79.2 10.5 all-gather.12
  140.0 86.5 all-reduce.4
  228.5 26.8 all-gather.14
  257.3 27.8 all-gather.16
  298.7 86.5 all-reduce.6
  386.8 148.5 all-gather.18
  633.0 7.8 reduce-scatter.6
  651.7 84.6 all-reduce.8
  740.4 50.3 reduce-scatter.14
  794.9 51.2 reduce-scatter.16
  850.0 35.9 reduce-scatter.12
  889.8 46.1 reduce-scatter.10
  940.3 61.7 reduce-scatter.8
